TPU v7x, 256 devices: a whole 4x4x8 slice. The times are simulated.
256 devices in a mesh: cfg: 2 (over core), seq: 64 (over x, z_hi, y), rep: 2 (over z_lo).
Axes of the slice: x: 4, y: 4, z: 8 (z_hi: 4, z_lo: 2; z = z_hi * 2 + z_lo), core: 2. Of those that a mesh axis runs over, the one named last changes fastest.
Arguments:
- queries: bfloat16 [2, 8192, 1536], P('cfg', 'seq', 'rep'), may hold values from -205 to 205
- keyvals: bfloat16 [2, 2, 8192, 1536], P('cfg', None, 'seq', 'rep'), may hold values from -13.5 to 13.5
- out_weight: bfloat16 [1536, 3072], P('rep', 'seq'), may hold values from -0.15625 to 0.15625
- latent: bfloat16 [8192, 3072], P('seq', ('cfg', 'rep')), may hold values from -6 to 6
- timestep: int32 [8192], P('seq'), may hold values from 0 to 49
- cond_mask: int32 [8192], P('seq'), may hold values 0 or 1
Outputs:
- denoised: bfloat16 [8192, 3072], P('seq', ('cfg', 'rep'))
All inputs are finite; a program needn't handle non-finite values. No bound on the sum of `cond_mask` on one device may be relied on, other than what follows from the above.
Results may differ from a plain program's by a relative error of at most 0.012.
Values may be sent and summed in bfloat16 or wider, within the bound.
A program may use at most 128 MiB of HBM per device.

v0:
```python
import math

import jax
import jax.numpy as jnp
from jax import lax
from jax.sharding import PartitionSpec as P

HD = 128
NSTEPS = 50


guide_scale = 3.0


def on_device(queries, keyvals, out_weight, latent, timestep, cond_mask):
    rows = queries.shape[1]
    local_width = queries.shape[2]
    local_heads = local_width // HD
    query_heads = queries[0].reshape(rows, local_heads, HD)
    piece = lax.all_gather(keyvals, "seq", axis=2, tiled=True)
    running_top = jnp.full((local_heads, rows), -1e30, jnp.float32)
    count = piece.shape[2]
    keys = piece[0, 0].reshape(count, local_heads, HD)
    values = piece[0, 1].reshape(count, local_heads, HD)
    scores = jnp.einsum(
        "rhd,khd->hrk", query_heads, keys, preferred_element_type=jnp.float32
    ) / math.sqrt(HD)
    new_top = jnp.maximum(running_top, jnp.max(scores, axis=-1))
    weights = jnp.exp(scores - new_top[:, :, None])
    new_total = jnp.sum(weights, axis=-1)
    mixed = jnp.einsum(
        "hrk,khd->rhd", weights.astype(jnp.bfloat16), values, preferred_element_type=jnp.float32
    )
    attended = mixed / jnp.transpose(new_total)[:, :, None]
    attended = attended.reshape(rows, local_width).astype(jnp.bfloat16)
    projected = jnp.dot(
        attended,
        lax.all_gather(out_weight, "seq", axis=1, tiled=True),
        preferred_element_type=jnp.float32,
    )
    factor_rows = 1.0 + (guide_scale - 1.0) * cond_mask.astype(jnp.float32)
    branch = lax.axis_index("cfg")
    branch_weight = jnp.where(branch == 0, factor_rows, 1.0 - factor_rows)
    weighted = projected * branch_weight[:, None]
    partial_cols = lax.psum_scatter(
        weighted.astype(jnp.bfloat16), "cfg", scatter_dimension=1, tiled=True
    )
    guided = lax.psum_scatter(partial_cols, "rep", scatter_dimension=1, tiled=True).astype(
        jnp.float32
    )
    sigma = 0.5 * jnp.exp(math.log(8.0) * timestep.astype(jnp.float32) / (NSTEPS - 1))
    return (latent.astype(jnp.float32) - sigma[:, None] * guided).astype(jnp.bfloat16)


def solution(mesh):
    placed = (
        P("cfg", "seq", "rep"),
        P("cfg", None, "seq", "rep"),
        P("rep", "seq"),
        P("seq", ("cfg", "rep")),
        P("seq"),
        P("seq"),
    )
    return jax.shard_map(
        on_device, mesh=mesh, in_specs=placed, out_specs=P("seq", ("cfg", "rep")), check_vma=False
    )
```

profile of v0, /device:TPU:1, one launch (start us, length us, event | category | flops | bytes accessed | tf_op | source)
XLA Modules:
  0.0 473.8 jit_solution(10063074028536511277)
XLA Ops:
  6.5 0.0 all-gather.3.cloned.1.call-start
  6.5 2.0 copy.10
  8.5 0.0 all-gather.3.cloned.1.call-update
  8.5 0.0 all-gather.5.cloned.1.call-start
  8.6 0.7 all-gather.5.cloned.1.call-update
  9.3 0.0 reduce-scatter.3.cloned.1.call-start
  9.3 1.1 copy.9
  10.4 0.7 broadcast_select_fusion
  11.1 321.9 %all-gather.3.cloned.1.call-done = bf16[1,2,8192,768]{2,3,1,0:T(8,128)(2,1)} async-done(((bf16[1,2,128,768]{2,3,1,0:T(8,128)(2,1)}), bf16[1,2,8192,768]{2,3,1,0:T(8,128)(2,1)}) %all-gather.3.cloned.1.call-update) | async-done | bytes 25165840 | tf_op jit(solution)/shard_map/all_gather | solution.py:20
  333.0 13.6 %fusion.17 = (bf16[1,1,8192,768]{2,3,1,0:T(8,128)(2,1)S(1)}, bf16[1,1,8192,768]{2,3,1,0:T(8,128)(2,1)}) fusion(bf16[1,2,8192,768]{2,3,1,0:T(8,128)(2,1)} %all-gather.3.cloned.1.call-done), kind=kLoop, calls=%fused_computation.17 | loop fusion | bytes 50331648 | tf_op jit(solution)/shard_map/slice | solution.py:23
  346.6 10.1 %multiply_reduce_fusion = (f32[6,128]{1,0:T(8,128)S(1)}, f32[6,128,8192]{2,1,0:T(8,128)}) fusion(bf16[128,6,128]{0,2,1:T(8,128)(2,1)S(1)} %bitcast.18, bf16[8192,6,128]{0,2,1:T(8,128)(2,1)S(1)} %bitcast.16), kind=kOutput, calls=%fused_computation.1 | convolution fusion | flops 1623194880 | bytes 37948416 | tf_op jit(solution)/shard_map/rhd,khd->hrk/dot_general | solution.py:25
  356.7 10.8 %fusion = f32[6,128]{1,0:T(8,128)S(1)} fusion(f32[6,128,8192]{2,1,0:T(8,128)} %get-tuple-element.8, f32[6,128]{1,0:T(8,128)S(1)} %broadcast_maximum_fusion), kind=kLoop, calls=%fused_computation.2 | loop fusion | flops 18873600 | bytes 25171968 | tf_op jit(solution)/shard_map/reduce_sum | solution.py:30
  367.6 0.0 copy-start.1
  367.6 0.0 copy-start
  367.6 14.7 %fusion.13 = bf16[128,6,128]{0,2,1:T(8,128)(2,1)S(1)} fusion(bf16[8192,6,128]{0,2,1:T(8,128)(2,1)} %bitcast.17, f32[6,128,8192]{2,1,0:T(8,128)} %get-tuple-element.8, f32[6,128]{1,0:T(8,128)S(1)} %broadcast_maximum_fusion, f32[128,6]{0,1:T(8,128)S(1)} %bitcast.20), kind=kOutput, calls=%fused_computation.11 | convolution fusion | flops 1629683712 | bytes 37951488 | tf_op jit(solution)/shard_map/hrk,khd->rhd/dot_general | solution.py:31
  382.3 44.6 %all-gather.5.cloned.1.call-done = bf16[768,3072]{0,1:T(8,128)(2,1)} async-done(((bf16[768,48]{0,1:T(8,128)(2,1)}), bf16[768,3072]{0,1:T(8,128)(2,1)}) %all-gather.5.cloned.1.call-update) | async-done | bytes 4718608 | tf_op jit(solution)/shard_map/all_gather | solution.py:38
  426.9 4.9 %fusion.6 = bf16[128,3072]{1,0:T(8,128)(2,1)} fusion(bf16[128,768]{0,1:T(8,128)(2,1)S(1)} %bitcast.19, bf16[768,3072]{0,1:T(8,128)(2,1)} %all-gather.5.cloned.1.call-done, f32[128]{0:T(128)S(1)} %broadcast_select_fusion), kind=kOutput, calls=%fused_computation.8 | convolution fusion | flops 604766208 | bytes 5702144 | tf_op jit(solution)/shard_map/dot_general | solution.py:36
  431.8 0.0 reduce-scatter.3.cloned.1.call-update
  431.8 0.0 reduce-scatter.5.cloned.1.call-start
  431.8 12.6 %reduce-scatter.3.cloned.1.call-done = bf16[128,1536]{1,0:T(8,128)(2,1)} async-done(((bf16[128,3072]{1,0:T(8,128)(2,1)}), bf16[128,1536]{1,0:T(8,128)(2,1)}) %reduce-scatter.3.cloned.1.call-update) | async-done | bytes 393232 | tf_op jit(solution)/shard_map/reduce_scatter | solution.py:45
  444.5 0.0 reduce-scatter.5.cloned.1.call-update
  444.5 0.0 copy-done.1
  444.5 21.0 %reduce-scatter.5.cloned.1.call-done = bf16[128,768]{1,0:T(8,128)(2,1)} async-done(((bf16[128,1536]{1,0:T(8,128)(2,1)}), bf16[128,768]{1,0:T(8,128)(2,1)}) %reduce-scatter.5.cloned.1.call-update) | async-done | bytes 196624 | tf_op jit(solution)/shard_map/reduce_scatter | solution.py:48
  465.6 0.0 copy-done
  465.6 1.7 subtract_convert_fusion
  (2 shorter events, 0.0 us)
Async XLA Ops:
  6.5 326.4 %all-gather.3.cloned.1.call-start = ((), (), s32[]{:S(2)}) async-start(), calls=%async_computation.2 | async-start | bytes 25559040 | tf_op jit(solution)/shard_map/all_gather | solution.py:20
  8.5 418.3 %all-gather.5.cloned.1.call-start = ((), (), s32[]{:S(2)}) async-start(), calls=%async_computation.3 | async-start | bytes 4792320 | tf_op jit(solution)/shard_map/all_gather | solution.py:38
  9.3 435.2 %reduce-scatter.3.cloned.1.call-start = ((), (), s32[]{:S(2)}) async-start(), calls=%async_computation.4 | async-start | bytes 1179648 | tf_op jit(solution)/shard_map/reduce_scatter | solution.py:45
  367.6 76.9 %copy-start.1 = (s32[128]{0:T(128)S(1)}, s32[128]{0:T(128)}, u32[]{:S(2)}) copy-start(s32[128]{0:T(128)} %param.10) | copy-start | bytes 1540
  367.6 98.0 %copy-start = (bf16[128,768]{1,0:T(8,128)(2,1)S(1)}, bf16[128,768]{1,0:T(8,128)(2,1)}, u32[]{:S(2)}) copy-start(bf16[128,768]{1,0:T(8,128)(2,1)} %param.9) | copy-start | bytes 589828
  431.8 33.8 %reduce-scatter.5.cloned.1.call-start = ((), (), s32[]{:S(2)}) async-start(), calls=%async_computation.5 | async-start | bytes 589824 | tf_op jit(solution)/shard_map/reduce_scatter | solution.py:48
Sparse Core Ops, SparseCore 0:
  10.4 322.4 all-gather.2
  336.2 90.6 all-gather.4
  431.9 12.5 reduce-scatter.2
  446.8 18.6 reduce-scatter.4
where the time goes:
time: 474 us
  waiting for transfers between devices  401 us (85%)
  matrix products  29.7 us (6%)
  local copies, waits for them, and re-layouts  16.7 us (4%)
  other arithmetic  13.2 us (3%)
  between operations  13.2 us (3%)
    all_gather x1, waiting for transfers between devices, on_device(): piece = lax.all_gather(keyvals, 'seq', axis=2, tiled=True)  322 us
    all_gather x1, waiting for transfers between devices, on_device(): lax.all_gather(out_weight, 'seq', axis=1, tiled=True)  44.6 us
    reduce_scatter x1, waiting for transfers between devices, on_device(): lax.psum_scatter(partial_cols, 'rep', scatter_dimension=1, tiled=True)  21 us
    dot_general x1, matrix products, on_device(): jnp.einsum('hrk,khd->rhd', weights.astype(jnp.bfloat16), values, preferre...  14.7 us
    slice x1, local copies, waits for them, and re-layouts, on_device(): keys = piece[0, 0].reshape(count, local_heads, HD)  13.6 us
    reduce_scatter x1, waiting for transfers between devices, on_device(): lax.psum_scatter(weighted.astype(jnp.bfloat16), 'cfg', scatter_dimension=...  12.6 us
    reduce_sum x1, other arithmetic, on_device(): new_total = jnp.sum(weights, axis=-1)  10.8 us
    dot_general x1, matrix products, on_device(): jnp.einsum('rhd,khd->hrk', query_heads, keys, preferred_element_type=jnp....  10.1 us
  transfers between devices with their start and end apart: 4, of which 4 were waited for; matrix products, arithmetic and copies ran while one was open for 11% of the time, Pallas kernels for 0%

commit v1 on v0

v1 whole, which is shorter than its diff:
```python
import math

import jax
import jax.numpy as jnp
from jax import lax
from jax.experimental import pallas as pl
from jax.experimental.pallas import tpu as pltpu
from jax.sharding import PartitionSpec as P

HD = 128
NSTEPS = 50
guide_scale = 3.0
SCALE = math.log2(math.e) / math.sqrt(HD)
MESH = pl.DeviceIdType.MESH
F32 = jnp.float32
BF16 = jnp.bfloat16


def dot_t(a, b):
    return lax.dot_general(a, b, (((1,), (1,)), ((), ())), preferred_element_type=F32)


def rcopy(src, dst, send_sem, recv_sem, device):
    return pltpu.make_async_remote_copy(
        src_ref=src, dst_ref=dst, send_sem=send_sem, recv_sem=recv_sem,
        device_id=device, device_id_type=MESH,
    )


def kernel(q_in, kv_in, w_in, mask_in, out_ref,
           kv, qb, osend, opart, lsend, lpart, ored, oz, cmb, wt, wb,
           sz, sy, ss, sx, so, sl, sr, sc, sw,
           rt, rq, ry, rs, rx, ro, rl, rz, rc, rwa, rw):
    c = lax.axis_index("cfg")
    s = lax.axis_index("seq")
    r = lax.axis_index("rep")
    x, k, y = s // 16, (s // 4) % 4, s % 4

    def dev(c_, x_, k_, y_, r_):
        return (c_, x_ * 16 + k_ * 4 + y_, r_)

    def xdev(d):
        return dev(c, (x + d) % 4, k, y, r)

    def ydev(d):
        return dev(c, x, k, (y + d) % 4, r)

    def zdev(d):
        return dev(c, x, (k + d) % 4, y, r)

    wdx, wsx = 2 * r + c, 2 * c + r
    wdest = dev(x // 2, wdx, k, y, x % 2)
    wsrc = dev(x % 2, wsx, k, y, x // 2)
    wself = jnp.logical_and(jnp.logical_and(wdx == x, x // 2 == c), x % 2 == r)

    barrier = pltpu.get_barrier_semaphore()

    def hello(device):
        pl.semaphore_signal(barrier, inc=1, device_id=device, device_id_type=MESH)

    for d in range(1, 4):
        hello(xdev(d))
        hello(ydev(d))
        hello(zdev(d))
    for d in range(4):
        hello(dev(1 - c, x, (k + d) % 4, y, r))
    hello(dev(c, x, k, y, 1 - r))
    hello(dev(1 - c, x, k, y, 1 - r))

    @pl.when(jnp.logical_not(wself))
    def _():
        hello(wdest)
        hello(wsrc)

    eye48 = jnp.where(
        lax.broadcasted_iota(jnp.int32, (48, 48), 0) == lax.broadcasted_iota(jnp.int32, (48, 48), 1), 1.0, 0.0
    ).astype(BF16)
    wt[...] = dot_t(eye48, w_in[...]).astype(BF16)
    eye = lax.broadcasted_iota(jnp.int32, (128, 128), 0) == lax.broadcasted_iota(jnp.int32, (128, 128), 1)

    def to_row(col):
        return jnp.sum(jnp.where(eye, jnp.broadcast_to(col, (128, 128)), 0.0), axis=0, keepdims=True)

    def to_col(row):
        return jnp.sum(jnp.where(eye, jnp.broadcast_to(row, (128, 128)), 0.0), axis=1, keepdims=True)

    pl.semaphore_wait(barrier, jnp.where(wself, 15, 17))

    def z_copies(j, q, t):
        kd = 2 * c + q
        lanes = pl.ds(384 * q + 128 * j, 128)
        if t == 2:
            core = k // 2
            return (q_in.at[:, lanes], qb.at[j, x, k % 2], rq.at[j], core, kd, kd == k)
        return (kv_in.at[t, :, lanes], kv.at[t, j, y, k], rt.at[j], t, kd, jnp.logical_and(kd == k, c == t))

    def z_remote(j, q, t):
        src, dst, sem, core, kd, same = z_copies(j, q, t)
        return rcopy(src, dst, sz.at[j, q, t], sem, dev(core, x, kd, y, r)), src, dst, sem, same

    for j in range(3):
        for t in (2, 0, 1):
            for q in range(2):
                copy, src, dst, sem, same = z_remote(j, q, t)

                @pl.when(same)
                def _():
                    pltpu.make_async_copy(src, dst, sem).start()

                @pl.when(jnp.logical_not(same))
                def _():
                    copy.start()

    wcopy = rcopy(wt.at[:, pl.ds(pl.multiple_of(384 * c, 128), 384)],
                  wb.at[k, y, :, pl.ds(pl.multiple_of(384 * wdx, 128), 384)], sw.at[0], rwa, wdest)
    my_lanes = pl.ds(pl.multiple_of(384 * x, 128), 384)

    @pl.when(wself)
    def _():
        pltpu.make_async_copy(wt.at[:, pl.ds(pl.multiple_of(384 * c, 128), 384)],
                              wb.at[k, y, :, my_lanes], rwa).start()

    @pl.when(jnp.logical_not(wself))
    def _():
        wcopy.start()

    def x_copy(j, d):
        return rcopy(qb.at[j, x], qb.at[j, x], sx.at[j, d], rx.at[j, d], xdev(d))

    def x_wait(j, d):
        src = (x + 4 - d) % 4
        rcopy(qb.at[j, src], qb.at[j, src], sx.at[j, d], rx.at[j, d], xdev(d)).wait_recv()

    def y_copy(j, d):
        return rcopy(kv.at[c, j, y], kv.at[c, j, y], sy.at[j, d], ry.at[j, d], ydev(d))

    def y_wait(j, d):
        src = (y + 4 - d) % 4
        rcopy(kv.at[c, j, src], kv.at[c, j, src], sy.at[j, d], ry.at[j, d], ydev(d)).wait_recv()

    def s_copy(j, d):
        src = (y + 4 - d) % 4
        return rcopy(kv.at[c, j, src], kv.at[c, j, src], ss.at[j, d], rs.at[j, d], dev(1 - c, x, k, y, r))

    def s_wait(j, d):
        src = (y + 4 - d) % 4
        rcopy(kv.at[1 - c, j, src], kv.at[1 - c, j, src], ss.at[j, d], rs.at[j, d],
              dev(1 - c, x, k, y, r)).wait_recv()

    def relay(j):
        rcopy(qb.at[j, x], qb.at[j, x], sx.at[j, 0], rq.at[j], xdev(1)).wait_recv()
        for d in (1, 3, 2):
            x_copy(j, d).start()
        rcopy(kv.at[c, j, y], kv.at[c, j, y], sx.at[j, 0], rt.at[j], ydev(1)).wait_recv()
        for d in (1, 3, 2):
            y_copy(j, d).start()
        s_copy(j, 0).start()

    def share(j):
        for d in (1, 3, 2):
            y_wait(j, d)
            s_copy(j, d).start()

    lo, hi = pl.ds(0, 2), pl.ds(2, 2)

    def wz(d):
        return rcopy(wb.at[k, y, :, my_lanes], wb.at[k, y, :, my_lanes], sw.at[d], rw.at[0, d], zdev(d))

    def wz_wait(d):
        kk = (k + 4 - d) % 4
        rcopy(wb.at[kk, y, :, my_lanes], wb.at[kk, y, :, my_lanes], sw.at[d], rw.at[0, d], zdev(d)).wait_recv()

    def lanes_of(xx):
        return pl.ds(pl.multiple_of(384 * xx, 128), 384)

    def wa2(d, yy):
        return rcopy(wb.at[lo, yy, :, my_lanes], wb.at[lo, yy, :, my_lanes], sw.at[3 + d], rw.at[1, d], ydev(d))

    def wb2(d, xx):
        return rcopy(wb.at[hi, y, :, lanes_of(xx)], wb.at[hi, y, :, lanes_of(xx)], sw.at[6 + d], rw.at[2, d], xdev(d))

    def wa3(d, xx):
        return rcopy(wb.at[lo, :, :, lanes_of(xx)], wb.at[lo, :, :, lanes_of(xx)], sw.at[9 + d], rw.at[3, d], xdev(d))

    def wb3(d, yy):
        return rcopy(wb.at[hi, yy], wb.at[hi, yy], sw.at[12 + d], rw.at[4, d], ydev(d))

    def w_first():
        rcopy(wb.at[k, y, :, my_lanes], wb.at[k, y, :, my_lanes], sw.at[0], rwa, wdest).wait_recv()
        for d in (1, 3, 2):
            wz(d).start()

    def w_second():
        for d in (1, 3, 2):
            wz_wait(d)
        for d in (1, 3, 2):
            wa2(d, y).start()
            wb2(d, x).start()

    def w_third():
        for d in (1, 3, 2):
            wa2(d, (y + 4 - d) % 4).wait_recv()
            wb2(d, (x + 4 - d) % 4).wait_recv()
        for d in (1, 3, 2):
            wa3(d, x).start()
            wb3(d, y).start()

    def w_last():
        for d in (1, 3, 2):
            wa3(d, (x + 4 - d) % 4).wait_recv()
            wb3(d, (y + 4 - d) % 4).wait_recv()

    def o_copy(j, d):
        return rcopy(osend.at[j, d], opart.at[j, d], so.at[j, d], ro.at[j, d], xdev(4 - d))

    def l_copy(j, d):
        return rcopy(lsend.at[j, d], lpart.at[j, d], sl.at[j, d], rl.at[j, d], xdev(4 - d))

    def compute(j):
        for d in range(4):
            s_wait(j, d)
        for d in range(1, 4):
            x_wait(j, d)

        def tile(d):
            qq = qb[j, (x + 4 - d) % 4].reshape(256, HD)
            scores = dot_t(qq, kv[0, j].reshape(2048, HD))
            top = jnp.max(scores, axis=1, keepdims=True)
            weights = jnp.exp2((scores - top) * SCALE)
            total = jnp.sum(weights, axis=1, keepdims=True)
            mixed = jnp.dot(weights.astype(BF16), kv[1, j].reshape(2048, HD), preferred_element_type=F32)
            osend[j, d] = (mixed * (1.0 / total)).astype(BF16)
            level = top * SCALE + jnp.log2(total)
            lsend[j, d] = jnp.concatenate(
                [jnp.broadcast_to(to_row(level[:128]), (4, 128)), jnp.broadcast_to(to_row(level[128:]), (4, 128))],
                axis=0,
            )

        def pair(u, carry):
            d0, d1 = 2 * u + 1, (2 * u + 2) % 4
            tile(d0)
            tile(d1)
            o_copy(j, d0).start()
            l_copy(j, d0).start()

            @pl.when(u == 0)
            def _():
                o_copy(j, d1).start()
                l_copy(j, d1).start()

            return carry

        lax.fori_loop(0, 2, pair, 0)

    oq = k % 2
    ob = k // 2

    def r_copy(j, h):
        return rcopy(ored.at[j, h], oz.at[ob, j], sr.at[j, h], rz.at[ob, j], dev(oq, x, 2 * c + h, y, r))

    def r_same(h):
        return jnp.logical_and(2 * c + h == k, oq == c)

    def merge(j):
        for d in range(1, 4):
            o_copy(j, d).wait_recv()
            l_copy(j, d).wait_recv()
        levels = [lsend[j, 0]] + [lpart[j, d] for d in range(1, 4)]
        best = jnp.maximum(jnp.maximum(levels[0], levels[1]), jnp.maximum(levels[2], levels[3]))
        parts = [jnp.exp2(v - best) for v in levels]
        inv = 1.0 / (parts[0] + parts[1] + parts[2] + parts[3])
        for h in range(2):
            total = None
            for d in range(4):
                share_d = to_col((parts[d] * inv)[4 * h:4 * h + 1])
                rows = pl.ds(128 * h, 128)
                block = osend[j, 0, rows, :] if d == 0 else opart[j, d, rows, :]
                term = block.astype(F32) * share_d
                total = term if total is None else total + term
            ored[j, h] = total.astype(BF16)
        for h in range(2):
            @pl.when(r_same(h))
            def _():
                pltpu.make_async_copy(ored.at[j, h], oz.at[ob, j], rz.at[ob, j]).start()

            @pl.when(jnp.logical_not(r_same(h)))
            def _():
                r_copy(j, h).start()

    factor = 1.0 + (guide_scale - 1.0) * to_col(mask_in[...].astype(F32))

    def c_lanes(rr, qq, j):
        return pl.ds(pl.multiple_of(128 * (6 * rr + 3 * qq + j), 128), 128)

    def c_peer(n):
        return (c if n == 1 else 1 - c), (r if n == 0 else 1 - r)

    def c_copy(j, n):
        cc, rr = c_peer(n)
        lanes = c_lanes(r, c, j)
        return rcopy(cmb.at[:, lanes], cmb.at[:, lanes], sc.at[j, n], rc.at[j, n], dev(cc, x, k, y, rr))

    def c_wait(j, n):
        cc, rr = c_peer(n)
        lanes = c_lanes(rr, cc, j)
        rcopy(cmb.at[:, lanes], cmb.at[:, lanes], sc.at[j, n], rc.at[j, n], dev(cc, x, k, y, rr)).wait_recv()

    def combine(j):
        for b in range(2):
            rcopy(oz.at[b, j], oz.at[b, j], sr.at[j, 0], rz.at[b, j], dev(1 - c, x, k, y, r)).wait_recv()
        guided = factor * oz[0, j].astype(F32) + (1.0 - factor) * oz[1, j].astype(F32)
        cmb[:, c_lanes(r, c, j)] = guided.astype(BF16)
        for n in (1, 2, 0):
            c_copy(j, n).start()

    relay(0)
    w_first()
    relay(1)
    share(0)
    relay(2)
    compute(0)
    share(1)
    w_second()
    compute(1)
    merge(0)
    share(2)
    w_third()
    compute(2)
    combine(0)
    merge(1)
    combine(1)
    merge(2)
    combine(2)
    for j in range(3):
        for n in range(3):
            c_wait(j, n)
    w_last()
    out_ref[...] = dot_t(cmb[...], wb[...].reshape(768, 1536))

    for j in range(3):
        for q in range(2):
            for t in range(3):
                copy, _src, _dst, _sem, same = z_remote(j, q, t)

                @pl.when(jnp.logical_not(same))
                def _():
                    copy.wait_send()

        for d in range(1, 4):
            x_copy(j, d).wait_send()
            y_copy(j, d).wait_send()
            o_copy(j, d).wait_send()
            l_copy(j, d).wait_send()
        for d in range(4):
            s_copy(j, d).wait_send()
        for h in range(2):
            @pl.when(jnp.logical_not(r_same(h)))
            def _():
                r_copy(j, h).wait_send()

        for n in range(3):
            c_copy(j, n).wait_send()

    @pl.when(jnp.logical_not(wself))
    def _():
        wcopy.wait_send()

    for d in range(1, 4):
        wz(d).wait_send()
        wa2(d, y).wait_send()
        wb2(d, x).wait_send()
        wa3(d, x).wait_send()
        wb3(d, y).wait_send()


def on_device(queries, keyvals, out_weight, latent, timestep, cond_mask):
    rows = queries.shape[1]
    dma = pltpu.SemaphoreType.DMA
    vmem = pltpu.VMEM
    guided = pl.pallas_call(
        kernel,
        out_shape=jax.ShapeDtypeStruct((rows, 768), F32),
        in_specs=[pl.BlockSpec(memory_space=vmem)] * 4,
        out_specs=pl.BlockSpec(memory_space=vmem),
        scratch_shapes=[
            vmem((2, 3, 4, 4, 128, HD), BF16),
            vmem((3, 4, 2, 128, HD), BF16),
            vmem((3, 4, 256, HD), BF16),
            vmem((3, 4, 256, HD), BF16),
            vmem((3, 4, 8, 128), F32),
            vmem((3, 4, 8, 128), F32),
            vmem((3, 2, 128, HD), BF16),
            vmem((2, 3, 128, HD), BF16),
            vmem((128, 1536), BF16),
            vmem((48, 768), BF16),
            vmem((4, 4, 48, 1536), BF16),
            dma((3, 2, 3)), dma((3, 4)), dma((3, 4)), dma((3, 4)), dma((3, 4)), dma((3, 4)),
            dma((3, 2)), dma((3, 3)), dma((16,)),
            dma((3,)), dma((3,)), dma((3, 4)), dma((3, 4)), dma((3, 4)), dma((3, 4)), dma((3, 4)),
            dma((2, 3)), dma((3, 3)), dma, dma((5, 4)),
        ],
        compiler_params=pltpu.CompilerParams(
            collective_id=0, has_side_effects=True, vmem_limit_bytes=58 << 20
        ),
    )(queries[0], keyvals[0], out_weight, cond_mask.reshape(1, rows))
    sigma = 0.5 * jnp.exp(math.log(8.0) * timestep.astype(F32) / (NSTEPS - 1))
    return (latent.astype(F32) - sigma[:, None] * guided).astype(BF16)


def solution(mesh):
    placed = (
        P("cfg", "seq", "rep"),
        P("cfg", None, "seq", "rep"),
        P("rep", "seq"),
        P("seq", ("cfg", "rep")),
        P("seq"),
        P("seq"),
    )
    return jax.shard_map(
        on_device, mesh=mesh, in_specs=placed, out_specs=P("seq", ("cfg", "rep")), check_vma=False
    )
```

time: 474 us -> 76 us (0.16)
  waiting for transfers between devices: 401 us -> 0 us
  Pallas kernels: 0 us -> 71.7 us
  matrix products: 29.7 us -> 0 us
  local copies, waits for them, and re-layouts: 16.7 us -> 2.36 us
  between operations: 13.2 us -> 0.02 us
  other arithmetic: 13.2 us -> 1.79 us
    all_gather x2 -> x0, waiting for transfers between devices: 366 us -> none  [the longest x1 322 us: on_device(): piece = lax.all_gather(keyvals, 'seq', axis=2, tiled=True)]
    pallas_call x0 -> x1, Pallas kernels: none -> 71.7 us  [on_device(): pl.pallas_call(kernel, out_shape=jax.ShapeDtypeStruct((rows, 768), F32),...]
    reduce_scatter x2 -> x0, waiting for transfers between devices: 33.7 us -> none  [the longest x1 21 us: on_device(): lax.psum_scatter(partial_cols, 'rep', scatter_dimension=1, tiled=True)]
    dot_general x3 -> x0, matrix products: 29.7 us -> none  [the longest x1 14.7 us: on_device(): jnp.einsum('hrk,khd->rhd', weights.astype(jnp.bfloat16), values, preferre...]
    slice x1 -> x0, local copies, waits for them, and re-layouts: 13.6 us -> none  [on_device(): keys = piece[0, 0].reshape(count, local_heads, HD)]
    reduce_sum x1 -> x0, other arithmetic: 10.8 us -> none  [on_device(): new_total = jnp.sum(weights, axis=-1)]
  transfers between devices with their start and end apart: 4 -> 0, of which waited for: 4 -> 0; matrix products, arithmetic and copies ran while one was open for 11% -> 0% of each run, Pallas kernels for 0% -> 0%
where the time goes in v1:
time: 76 us; the launch traced here: 75.9 us
  Pallas kernels  71.7 us (94%)
  local copies, waits for them, and re-layouts  2.36 us (3%)
  other arithmetic  1.79 us (2%)
    pallas_call x1, Pallas kernels, on_device(): pl.pallas_call(kernel, out_shape=jax.ShapeDtypeStruct((rows, 768), F32),...  71.7 us
    unnamed x5, local copies, waits for them, and re-layouts  2.36 us
    convert_element_type x1, other arithmetic, on_device(): return (latent.astype(F32) - sigma[:, None] * guided).astype(BF16)  1.79 us

profile of v1, /device:TPU:1, one launch (start us, length us, event | category | flops | bytes accessed | tf_op | source)
XLA Modules:
  0.0 75.9 jit_solution(17635929670335850256)
XLA Ops:
  0.0 0.0 copy-start.1
  0.0 0.7 copy-done.1
  0.7 1.7 %copy.7.w_in = bf16[768,48]{1,0:T(8,128)(2,1)} copy(bf16[768,48]{0,1:T(8,128)(2,1)} %param.8) | data formatting | bytes 147456 | tf_op args[2]
  2.4 0.0 copy-start
  2.4 71.7 %shard_map.64 = f32[128,768]{1,0:T(8,128)} custom-call(bf16[128,768]{1,0:T(8,128)(2,1)} %bitcast.4, bf16[2,128,768]{2,1,0:T(8,128)(2,1)} %bitcast.3, bf16[768,48]{1,0:T(8,128)(2,1)} %copy.7.w_in, s32[1,128]{1,0:T(1,128)} %bitcast.5), custom_call_target="tpu_custom_call" | custom-call | tf_op jit(solution)/shard_map/pallas_call | solution.py:380
  74.1 0.0 copy-done
  74.1 1.8 %subtract_convert_fusion = bf16[128,768]{1,0:T(8,128)(2,1)} fusion(f32[128,768]{1,0:T(8,128)} %shard_map.64, bf16[128,768]{1,0:T(8,128)(2,1)S(1)} %copy-done, f32[128]{0:T(128)S(1)} %exponential_multiply_fusion), kind=kLoop, calls=%fused_computation | loop fusion | flops 393216 | bytes 786944 | tf_op jit(solution)/shard_map/convert_element_type | solution.py:407
  (1 shorter events, 0.0 us)
Async XLA Ops:
  0.0 0.7 copy-start.1
  2.4 71.7 %copy-start = (bf16[128,768]{1,0:T(8,128)(2,1)S(1)}, bf16[128,768]{1,0:T(8,128)(2,1)}, u32[]{:S(2)}) copy-start(bf16[128,768]{1,0:T(8,128)(2,1)} %param.9) | copy-start | bytes 589828

commit v2 on v1

--- a/solution.py
+++ b/solution.py
@@ -27,10 +27,10 @@
     )
 
 
-def kernel(q_in, kv_in, w_in, mask_in, out_ref,
-           kv, qb, osend, opart, lsend, lpart, ored, oz, cmb, wt, wb,
+def kernel(q_hbm, kv_hbm, w_hbm, latent_hbm, step_in, mask_in, out_ref,
+           q_in, kv_in, wt, lat, kv, qb, osend, opart, lsend, lpart, ored, oz, cmb, wb,
            sz, sy, ss, sx, so, sl, sr, sc, sw,
-           rt, rq, ry, rs, rx, ro, rl, rz, rc, rwa, rw):
+           rt, rq, ry, rs, rx, ro, rl, rz, rc, rwa, rw, sin):
     c = lax.axis_index("cfg")
     s = lax.axis_index("seq")
     r = lax.axis_index("rep")
@@ -72,10 +72,12 @@
         hello(wdest)
         hello(wsrc)
 
-    eye48 = jnp.where(
-        lax.broadcasted_iota(jnp.int32, (48, 48), 0) == lax.broadcasted_iota(jnp.int32, (48, 48), 1), 1.0, 0.0
-    ).astype(BF16)
-    wt[...] = dot_t(eye48, w_in[...]).astype(BF16)
+    staged = [
+        pltpu.make_async_copy(src, dst, sin.at[n])
+        for n, (src, dst) in enumerate(((q_hbm, q_in), (kv_hbm, kv_in), (w_hbm, wt), (latent_hbm, lat)))
+    ]
+    for copy in staged:
+        copy.start()
     eye = lax.broadcasted_iota(jnp.int32, (128, 128), 0) == lax.broadcasted_iota(jnp.int32, (128, 128), 1)
 
     def to_row(col):
@@ -84,15 +86,23 @@
     def to_col(row):
         return jnp.sum(jnp.where(eye, jnp.broadcast_to(row, (128, 128)), 0.0), axis=1, keepdims=True)
 
+    for copy in staged:
+        copy.wait()
     pl.semaphore_wait(barrier, jnp.where(wself, 15, 17))
+
+    def row_axis(j):
+        return (y, ydev) if j == 1 else (x, xdev)
+
+    def key_axis(j):
+        return (x, xdev) if j == 1 else (y, ydev)
 
     def z_copies(j, q, t):
         kd = 2 * c + q
         lanes = pl.ds(384 * q + 128 * j, 128)
         if t == 2:
             core = k // 2
-            return (q_in.at[:, lanes], qb.at[j, x, k % 2], rq.at[j], core, kd, kd == k)
-        return (kv_in.at[t, :, lanes], kv.at[t, j, y, k], rt.at[j], t, kd, jnp.logical_and(kd == k, c == t))
+            return (q_in.at[:, lanes], qb.at[j, row_axis(j)[0], k % 2], rq.at[j], core, kd, kd == k)
+        return (kv_in.at[t, :, lanes], kv.at[t, j, key_axis(j)[0], k], rt.at[j], t, kd, jnp.logical_and(kd == k, c == t))
 
     def z_remote(j, q, t):
         src, dst, sem, core, kd, same = z_copies(j, q, t)
@@ -112,81 +122,100 @@
                     copy.start()
 
     wcopy = rcopy(wt.at[:, pl.ds(pl.multiple_of(384 * c, 128), 384)],
-                  wb.at[k, y, :, pl.ds(pl.multiple_of(384 * wdx, 128), 384)], sw.at[0], rwa, wdest)
-    my_lanes = pl.ds(pl.multiple_of(384 * x, 128), 384)
+                  wb.at[wdx, k, y], sw.at[0], rwa, wdest)
 
     @pl.when(wself)
     def _():
         pltpu.make_async_copy(wt.at[:, pl.ds(pl.multiple_of(384 * c, 128), 384)],
-                              wb.at[k, y, :, my_lanes], rwa).start()
+                              wb.at[x, k, y], rwa).start()
 
     @pl.when(jnp.logical_not(wself))
     def _():
         wcopy.start()
 
-    def x_copy(j, d):
-        return rcopy(qb.at[j, x], qb.at[j, x], sx.at[j, d], rx.at[j, d], xdev(d))
+    near = 1 + 2 * c
+
+    def x_copy(j, d, src, to):
+        block = qb.at[j, src]
+        return rcopy(block, block, sx.at[j, d], rx.at[j, d], row_axis(j)[1](to))
+
+    def x_send(j, d):
+        return x_copy(j, d, row_axis(j)[0], d)
+
+    def x_pass(j):
+        return x_copy(j, 2, (row_axis(j)[0] + 4 - near) % 4, near)
 
     def x_wait(j, d):
-        src = (x + 4 - d) % 4
-        rcopy(qb.at[j, src], qb.at[j, src], sx.at[j, d], rx.at[j, d], xdev(d)).wait_recv()
-
-    def y_copy(j, d):
-        return rcopy(kv.at[c, j, y], kv.at[c, j, y], sy.at[j, d], ry.at[j, d], ydev(d))
+        x_copy(j, d, (row_axis(j)[0] + 4 - d) % 4, d).wait_recv()
+
+    def y_copy(j, d, src, to):
+        block = kv.at[c, j, src]
+        return rcopy(block, block, sy.at[j, d], ry.at[j, d], key_axis(j)[1](to))
+
+    def y_send(j, d):
+        return y_copy(j, d, key_axis(j)[0], d)
+
+    def y_pass(j):
+        return y_copy(j, 2, (key_axis(j)[0] + 4 - near) % 4, near)
 
     def y_wait(j, d):
-        src = (y + 4 - d) % 4
-        rcopy(kv.at[c, j, src], kv.at[c, j, src], sy.at[j, d], ry.at[j, d], ydev(d)).wait_recv()
+        y_copy(j, d, (key_axis(j)[0] + 4 - d) % 4, d).wait_recv()
 
     def s_copy(j, d):
-        src = (y + 4 - d) % 4
-        return rcopy(kv.at[c, j, src], kv.at[c, j, src], ss.at[j, d], rs.at[j, d], dev(1 - c, x, k, y, r))
+        block = kv.at[c, j, (key_axis(j)[0] + 4 - d) % 4]
+        return rcopy(block, block, ss.at[j, d], rs.at[j, d], dev(1 - c, x, k, y, r))
 
     def s_wait(j, d):
-        src = (y + 4 - d) % 4
-        rcopy(kv.at[1 - c, j, src], kv.at[1 - c, j, src], ss.at[j, d], rs.at[j, d],
-              dev(1 - c, x, k, y, r)).wait_recv()
+        block = kv.at[1 - c, j, (key_axis(j)[0] + 4 - d) % 4]
+        rcopy(block, block, ss.at[j, d], rs.at[j, d], dev(1 - c, x, k, y, r)).wait_recv()
 
     def relay(j):
-        rcopy(qb.at[j, x], qb.at[j, x], sx.at[j, 0], rq.at[j], xdev(1)).wait_recv()
-        for d in (1, 3, 2):
-            x_copy(j, d).start()
-        rcopy(kv.at[c, j, y], kv.at[c, j, y], sx.at[j, 0], rt.at[j], ydev(1)).wait_recv()
-        for d in (1, 3, 2):
-            y_copy(j, d).start()
+        own = qb.at[j, row_axis(j)[0]]
+        rcopy(own, own, sx.at[j, 0], rq.at[j], xdev(1)).wait_recv()
+        for d in (1, 3):
+            x_send(j, d).start()
+        own = kv.at[c, j, key_axis(j)[0]]
+        rcopy(own, own, sx.at[j, 0], rt.at[j], ydev(1)).wait_recv()
+        for d in (1, 3):
+            y_send(j, d).start()
         s_copy(j, 0).start()
 
+    def forward(j):
+        x_wait(j, near)
+        x_pass(j).start()
+        y_wait(j, near)
+        y_pass(j).start()
+        s_copy(j, near).start()
+        y_wait(j, 4 - near)
+        s_copy(j, 4 - near).start()
+
     def share(j):
-        for d in (1, 3, 2):
-            y_wait(j, d)
-            s_copy(j, d).start()
+        y_wait(j, 2)
+        s_copy(j, 2).start()
 
     lo, hi = pl.ds(0, 2), pl.ds(2, 2)
 
     def wz(d):
-        return rcopy(wb.at[k, y, :, my_lanes], wb.at[k, y, :, my_lanes], sw.at[d], rw.at[0, d], zdev(d))
+        return rcopy(wb.at[x, k, y], wb.at[x, k, y], sw.at[d], rw.at[0, d], zdev(d))
 
     def wz_wait(d):
         kk = (k + 4 - d) % 4
-        rcopy(wb.at[kk, y, :, my_lanes], wb.at[kk, y, :, my_lanes], sw.at[d], rw.at[0, d], zdev(d)).wait_recv()
-
-    def lanes_of(xx):
-        return pl.ds(pl.multiple_of(384 * xx, 128), 384)
+        rcopy(wb.at[x, kk, y], wb.at[x, kk, y], sw.at[d], rw.at[0, d], zdev(d)).wait_recv()
 
     def wa2(d, yy):
-        return rcopy(wb.at[lo, yy, :, my_lanes], wb.at[lo, yy, :, my_lanes], sw.at[3 + d], rw.at[1, d], ydev(d))
+        return rcopy(wb.at[x, lo, yy], wb.at[x, lo, yy], sw.at[3 + d], rw.at[1, d], ydev(d))
 
     def wb2(d, xx):
-        return rcopy(wb.at[hi, y, :, lanes_of(xx)], wb.at[hi, y, :, lanes_of(xx)], sw.at[6 + d], rw.at[2, d], xdev(d))
+        return rcopy(wb.at[xx, hi, y], wb.at[xx, hi, y], sw.at[6 + d], rw.at[2, d], xdev(d))
 
     def wa3(d, xx):
-        return rcopy(wb.at[lo, :, :, lanes_of(xx)], wb.at[lo, :, :, lanes_of(xx)], sw.at[9 + d], rw.at[3, d], xdev(d))
+        return rcopy(wb.at[xx, lo], wb.at[xx, lo], sw.at[9 + d], rw.at[3, d], xdev(d))
 
     def wb3(d, yy):
-        return rcopy(wb.at[hi, yy], wb.at[hi, yy], sw.at[12 + d], rw.at[4, d], ydev(d))
+        return rcopy(wb.at[:, hi, yy], wb.at[:, hi, yy], sw.at[12 + d], rw.at[4, d], ydev(d))
 
     def w_first():
-        rcopy(wb.at[k, y, :, my_lanes], wb.at[k, y, :, my_lanes], sw.at[0], rwa, wdest).wait_recv()
+        rcopy(wb.at[x, k, y], wb.at[x, k, y], sw.at[0], rwa, wdest).wait_recv()
         for d in (1, 3, 2):
             wz(d).start()
 
@@ -197,13 +226,17 @@
             wa2(d, y).start()
             wb2(d, x).start()
 
-    def w_third():
+    def w_third_y():
+        for d in (1, 3, 2):
+            wb2(d, (x + 4 - d) % 4).wait_recv()
+        for d in (1, 3, 2):
+            wb3(d, y).start()
+
+    def w_third_x():
         for d in (1, 3, 2):
             wa2(d, (y + 4 - d) % 4).wait_recv()
-            wb2(d, (x + 4 - d) % 4).wait_recv()
         for d in (1, 3, 2):
             wa3(d, x).start()
-            wb3(d, y).start()
 
     def w_last():
         for d in (1, 3, 2):
@@ -211,19 +244,19 @@
             wb3(d, (y + 4 - d) % 4).wait_recv()
 
     def o_copy(j, d):
-        return rcopy(osend.at[j, d], opart.at[j, d], so.at[j, d], ro.at[j, d], xdev(4 - d))
+        return rcopy(osend.at[j, d], opart.at[j, d], so.at[j, d], ro.at[j, d], row_axis(j)[1](4 - d))
 
     def l_copy(j, d):
-        return rcopy(lsend.at[j, d], lpart.at[j, d], sl.at[j, d], rl.at[j, d], xdev(4 - d))
+        return rcopy(lsend.at[j, d], lpart.at[j, d], sl.at[j, d], rl.at[j, d], row_axis(j)[1](4 - d))
 
     def compute(j):
         for d in range(4):
             s_wait(j, d)
-        for d in range(1, 4):
-            x_wait(j, d)
+        x_wait(j, 4 - near)
+        x_wait(j, 2)
 
         def tile(d):
-            qq = qb[j, (x + 4 - d) % 4].reshape(256, HD)
+            qq = qb[j, (row_axis(j)[0] + 4 - d) % 4].reshape(256, HD)
             scores = dot_t(qq, kv[0, j].reshape(2048, HD))
             top = jnp.max(scores, axis=1, keepdims=True)
             weights = jnp.exp2((scores - top) * SCALE)
@@ -287,6 +320,7 @@
             def _():
                 r_copy(j, h).start()
 
+    sigma = to_col(0.5 * jnp.exp(math.log(8.0) * step_in[...].astype(F32) / (NSTEPS - 1)))
     factor = 1.0 + (guide_scale - 1.0) * to_col(mask_in[...].astype(F32))
 
     def c_lanes(rr, qq, j):
@@ -316,26 +350,33 @@
     relay(0)
     w_first()
     relay(1)
+    forward(0)
     share(0)
     relay(2)
+    forward(1)
     compute(0)
     share(1)
+    forward(2)
     w_second()
     compute(1)
+    share(2)
+    w_third_y()
     merge(0)
-    share(2)
-    w_third()
     compute(2)
+    w_third_x()
+    merge(1)
     combine(0)
-    merge(1)
+    merge(2)
     combine(1)
-    merge(2)
     combine(2)
     for j in range(3):
         for n in range(3):
             c_wait(j, n)
     w_last()
-    out_ref[...] = dot_t(cmb[...], wb[...].reshape(768, 1536))
+    guided = dot_t(cmb[:, 0:384], wb[0].reshape(768, 384))
+    for n in range(1, 4):
+        guided += dot_t(cmb[:, 384 * n:384 * n + 384], wb[n].reshape(768, 384))
+    out_ref[...] = (lat[...].astype(F32) - sigma * guided).astype(BF16)
 
     for j in range(3):
         for q in range(2):
@@ -347,8 +388,8 @@
                     copy.wait_send()
 
         for d in range(1, 4):
-            x_copy(j, d).wait_send()
-            y_copy(j, d).wait_send()
+            x_copy(j, d, 0, 1).wait_send()
+            y_copy(j, d, 0, 1).wait_send()
             o_copy(j, d).wait_send()
             l_copy(j, d).wait_send()
         for d in range(4):
@@ -377,12 +418,17 @@
     rows = queries.shape[1]
     dma = pltpu.SemaphoreType.DMA
     vmem = pltpu.VMEM
-    guided = pl.pallas_call(
+    anywhere = pl.BlockSpec(memory_space=pl.ANY)
+    return pl.pallas_call(
         kernel,
-        out_shape=jax.ShapeDtypeStruct((rows, 768), F32),
-        in_specs=[pl.BlockSpec(memory_space=vmem)] * 4,
+        out_shape=jax.ShapeDtypeStruct((rows, 768), BF16),
+        in_specs=[anywhere] * 4 + [pl.BlockSpec(memory_space=vmem)] * 2,
         out_specs=pl.BlockSpec(memory_space=vmem),
         scratch_shapes=[
+            vmem((rows, 768), BF16),
+            vmem((2, rows, 768), BF16),
+            vmem((48, 768), BF16),
+            vmem((rows, 768), BF16),
             vmem((2, 3, 4, 4, 128, HD), BF16),
             vmem((3, 4, 2, 128, HD), BF16),
             vmem((3, 4, 256, HD), BF16),
@@ -392,19 +438,16 @@
             vmem((3, 2, 128, HD), BF16),
             vmem((2, 3, 128, HD), BF16),
             vmem((128, 1536), BF16),
-            vmem((48, 768), BF16),
-            vmem((4, 4, 48, 1536), BF16),
+            vmem((4, 4, 4, 48, 384), BF16),
             dma((3, 2, 3)), dma((3, 4)), dma((3, 4)), dma((3, 4)), dma((3, 4)), dma((3, 4)),
             dma((3, 2)), dma((3, 3)), dma((16,)),
             dma((3,)), dma((3,)), dma((3, 4)), dma((3, 4)), dma((3, 4)), dma((3, 4)), dma((3, 4)),
-            dma((2, 3)), dma((3, 3)), dma, dma((5, 4)),
+            dma((2, 3)), dma((3, 3)), dma, dma((5, 4)), dma((4,)),
         ],
         compiler_params=pltpu.CompilerParams(
             collective_id=0, has_side_effects=True, vmem_limit_bytes=58 << 20
         ),
-    )(queries[0], keyvals[0], out_weight, cond_mask.reshape(1, rows))
-    sigma = 0.5 * jnp.exp(math.log(8.0) * timestep.astype(F32) / (NSTEPS - 1))
-    return (latent.astype(F32) - sigma[:, None] * guided).astype(BF16)
+    )(queries[0], keyvals[0], out_weight.T, latent, timestep.reshape(1, rows), cond_mask.reshape(1, rows))
 
 
 def solution(mesh):

time: 76 us -> 70.3 us (0.925)
  Pallas kernels: 71.7 us -> 67.8 us
  other arithmetic: 1.79 us -> 0 us
    pallas_call x1, Pallas kernels: 71.7 us -> 67.8 us  [on_device(): pl.pallas_call(kernel, out_shape=jax.ShapeDtypeStruct((rows, 768), BF16),...]
    convert_element_type x1 -> x0, other arithmetic: 1.79 us -> none  [on_device(): return (latent.astype(F32) - sigma[:, None] * guided).astype(BF16)]
    unnamed x5 -> x1, local copies, waits for them, and re-layouts: 2.36 us -> 1.62 us
where the time goes in v2:
time: 70.3 us; the launch traced here: 69.4 us
  Pallas kernels  67.8 us (96%)
  local copies, waits for them, and re-layouts  1.62 us (2%)
    pallas_call x1, Pallas kernels, on_device(): pl.pallas_call(kernel, out_shape=jax.ShapeDtypeStruct((rows, 768), BF16),...  67.8 us
    unnamed x1, local copies, waits for them, and re-layouts  1.62 us

profile of v2, /device:TPU:1, one launch (start us, length us, event | category | flops | bytes accessed | tf_op | source)
XLA Modules:
  0.0 69.4 jit_solution(17397948330507186864)
XLA Ops:
  0.0 67.8 %shard_map.64 = bf16[128,768]{1,0:T(8,128)(2,1)} custom-call(bf16[128,768]{1,0:T(8,128)(2,1)} %bitcast.6, bf16[2,128,768]{2,1,0:T(8,128)(2,1)} %bitcast.5, bf16[48,768]{1,0:T(8,128)(2,1)} %bitcast.7, bf16[128,768]{1,0:T(8,128)(2,1)} %latent_hbm.1, s32[1,128]{1,0:T(1,128)} %bitcast.8, s32[1,128]{1,0:T(1,128)} %bitcast.9), custom_call_target="tpu_custom_call" | custom-call | tf_op jit(solution)/shard_map/pallas_call | solution.py:422
  67.8 1.6 %copy.8 = bf16[128,768]{1,0:T(8,128)(2,1)} copy(bf16[128,768]{1,0:T(8,128)(2,1)} %shard_map.64) | data formatting | bytes 393216

commit v3 on v2

--- a/solution.py
+++ b/solution.py
@@ -208,11 +208,13 @@
     def wb2(d, xx):
         return rcopy(wb.at[xx, hi, y], wb.at[xx, hi, y], sw.at[6 + d], rw.at[2, d], xdev(d))
 
-    def wa3(d, xx):
-        return rcopy(wb.at[xx, lo], wb.at[xx, lo], sw.at[9 + d], rw.at[3, d], xdev(d))
-
-    def wb3(d, yy):
-        return rcopy(wb.at[:, hi, yy], wb.at[:, hi, yy], sw.at[12 + d], rw.at[4, d], ydev(d))
+    def wa3(d, xx, n):
+        block = wb.at[xx, n]
+        return rcopy(block, block, sw.at[16 + 4 * n + d], rw.at[3 + n, d], xdev(d))
+
+    def wb3(d, yy, n):
+        block = wb.at[:, 2 + n, yy]
+        return rcopy(block, block, sw.at[24 + 4 * n + d], rw.at[5 + n, d], ydev(d))
 
     def w_first():
         rcopy(wb.at[x, k, y], wb.at[x, k, y], sw.at[0], rwa, wdest).wait_recv()
@@ -226,22 +228,27 @@
             wa2(d, y).start()
             wb2(d, x).start()
 
-    def w_third_y():
+    def w_wait_b2():
         for d in (1, 3, 2):
             wb2(d, (x + 4 - d) % 4).wait_recv()
-        for d in (1, 3, 2):
-            wb3(d, y).start()
-
-    def w_third_x():
+
+    def w_wait_a2():
         for d in (1, 3, 2):
             wa2(d, (y + 4 - d) % 4).wait_recv()
-        for d in (1, 3, 2):
-            wa3(d, x).start()
+
+    def w_y(n):
+        for d in (1, 3, 2):
+            wb3(d, y, n).start()
+
+    def w_x(n):
+        for d in (1, 3, 2):
+            wa3(d, x, n).start()
 
     def w_last():
         for d in (1, 3, 2):
-            wa3(d, (x + 4 - d) % 4).wait_recv()
-            wb3(d, (y + 4 - d) % 4).wait_recv()
+            for n in range(2):
+                wa3(d, (x + 4 - d) % 4, n).wait_recv()
+                wb3(d, (y + 4 - d) % 4, n).wait_recv()
 
     def o_copy(j, d):
         return rcopy(osend.at[j, d], opart.at[j, d], so.at[j, d], ro.at[j, d], row_axis(j)[1](4 - d))
@@ -360,10 +367,14 @@
     w_second()
     compute(1)
     share(2)
-    w_third_y()
     merge(0)
     compute(2)
-    w_third_x()
+    w_wait_b2()
+    w_wait_a2()
+    w_x(0)
+    w_y(0)
+    w_x(1)
+    w_y(1)
     merge(1)
     combine(0)
     merge(2)
@@ -410,8 +421,9 @@
         wz(d).wait_send()
         wa2(d, y).wait_send()
         wb2(d, x).wait_send()
-        wa3(d, x).wait_send()
-        wb3(d, y).wait_send()
+        for n in range(2):
+            wa3(d, x, n).wait_send()
+            wb3(d, y, n).wait_send()
 
 
 def on_device(queries, keyvals, out_weight, latent, timestep, cond_mask):
@@ -440,9 +452,9 @@
             vmem((128, 1536), BF16),
             vmem((4, 4, 4, 48, 384), BF16),
             dma((3, 2, 3)), dma((3, 4)), dma((3, 4)), dma((3, 4)), dma((3, 4)), dma((3, 4)),
-            dma((3, 2)), dma((3, 3)), dma((16,)),
+            dma((3, 2)), dma((3, 3)), dma((32,)),
             dma((3,)), dma((3,)), dma((3, 4)), dma((3, 4)), dma((3, 4)), dma((3, 4)), dma((3, 4)),
-            dma((2, 3)), dma((3, 3)), dma, dma((5, 4)), dma((4,)),
+            dma((2, 3)), dma((3, 3)), dma, dma((7, 4)), dma((4,)),
         ],
         compiler_params=pltpu.CompilerParams(
             collective_id=0, has_side_effects=True, vmem_limit_bytes=58 << 20

time: 70.3 us -> 69.6 us (0.990); the launches traced: 69.4 us -> 69.5 us
  no operation moved by 1% of the time
where the time goes in v3:
time: 69.6 us; the launch traced here: 69.5 us
  Pallas kernels  67.8 us (97%)
  local copies, waits for them, and re-layouts  1.62 us (2%)
    pallas_call x1, Pallas kernels, on_device(): pl.pallas_call(kernel, out_shape=jax.ShapeDtypeStruct((rows, 768), BF16),...  67.8 us
    unnamed x1, local copies, waits for them, and re-layouts  1.62 us

profile of v3, /device:TPU:1, one launch (start us, length us, event | category | flops | bytes accessed | tf_op | source)
XLA Modules:
  0.0 69.5 jit_solution(8229898913848368277)
XLA Ops:
  0.0 67.8 %shard_map.64 = bf16[128,768]{1,0:T(8,128)(2,1)} custom-call(bf16[128,768]{1,0:T(8,128)(2,1)} %bitcast.6, bf16[2,128,768]{2,1,0:T(8,128)(2,1)} %bitcast.5, bf16[48,768]{1,0:T(8,128)(2,1)} %bitcast.7, bf16[128,768]{1,0:T(8,128)(2,1)} %latent_hbm.1, s32[1,128]{1,0:T(1,128)} %bitcast.8, s32[1,128]{1,0:T(1,128)} %bitcast.9), custom_call_target="tpu_custom_call" | custom-call | tf_op jit(solution)/shard_map/pallas_call | solution.py:434
  67.8 1.6 %copy.8 = bf16[128,768]{1,0:T(8,128)(2,1)} copy(bf16[128,768]{1,0:T(8,128)(2,1)} %shard_map.64) | data formatting | bytes 393216

commit v4 on v3

--- a/solution.py
+++ b/solution.py
@@ -194,36 +194,62 @@
         s_copy(j, 2).start()
 
     lo, hi = pl.ds(0, 2), pl.ds(2, 2)
-
-    def wz(d):
-        return rcopy(wb.at[x, k, y], wb.at[x, k, y], sw.at[d], rw.at[0, d], zdev(d))
-
-    def wz_wait(d):
-        kk = (k + 4 - d) % 4
-        rcopy(wb.at[x, kk, y], wb.at[x, kk, y], sw.at[d], rw.at[0, d], zdev(d)).wait_recv()
+    main, rest = pl.ds(0, 40), pl.ds(40, 8)
+
+    def wz(d, kk):
+        block = wb.at[x, kk, y, main]
+        return rcopy(block, block, sw.at[d], rw.at[0, d], zdev(d))
 
     def wa2(d, yy):
-        return rcopy(wb.at[x, lo, yy], wb.at[x, lo, yy], sw.at[3 + d], rw.at[1, d], ydev(d))
+        block = wb.at[x, lo, yy, main]
+        return rcopy(block, block, sw.at[3 + d], rw.at[1, d], ydev(d))
 
     def wb2(d, xx):
-        return rcopy(wb.at[xx, hi, y], wb.at[xx, hi, y], sw.at[6 + d], rw.at[2, d], xdev(d))
+        block = wb.at[xx, hi, y, main]
+        return rcopy(block, block, sw.at[6 + d], rw.at[2, d], xdev(d))
 
     def wa3(d, xx, n):
-        block = wb.at[xx, n]
+        block = wb.at[xx, n, :, main]
         return rcopy(block, block, sw.at[16 + 4 * n + d], rw.at[3 + n, d], xdev(d))
 
     def wb3(d, yy, n):
-        block = wb.at[:, 2 + n, yy]
+        block = wb.at[:, 2 + n, yy, main]
         return rcopy(block, block, sw.at[24 + 4 * n + d], rw.at[5 + n, d], ydev(d))
+
+    def wc1(d, xx):
+        block = wb.at[xx, k, y, rest]
+        return rcopy(block, block, sw.at[32 + d], rw.at[7, d], xdev(d))
+
+    def wc2(d, yy):
+        block = wb.at[:, k, yy, rest]
+        return rcopy(block, block, sw.at[36 + d], rw.at[8, d], ydev(d))
+
+    def wc3(d, kk):
+        block = wb.at[:, kk, :, rest]
+        return rcopy(block, block, sw.at[40 + d], rw.at[9, d], zdev(d))
+
+    def w_rest():
+        for d in (1, 3, 2):
+            wc1(d, (x + 4 - d) % 4).wait_recv()
+        for d in (1, 3, 2):
+            wc2(d, y).start()
+
+    def w_rest_z():
+        for d in (1, 3, 2):
+            wc2(d, (y + 4 - d) % 4).wait_recv()
+        for d in (1, 3, 2):
+            wc3(d, k).start()
 
     def w_first():
         rcopy(wb.at[x, k, y], wb.at[x, k, y], sw.at[0], rwa, wdest).wait_recv()
         for d in (1, 3, 2):
-            wz(d).start()
+            wc1(d, x).start()
+        for d in (1, 3, 2):
+            wz(d, k).start()
 
     def w_second():
         for d in (1, 3, 2):
-            wz_wait(d)
+            wz(d, (k + 4 - d) % 4).wait_recv()
         for d in (1, 3, 2):
             wa2(d, y).start()
             wb2(d, x).start()
@@ -245,6 +271,8 @@
             wa3(d, x, n).start()
 
     def w_last():
+        for d in (1, 3, 2):
+            wc3(d, (k + 4 - d) % 4).wait_recv()
         for d in (1, 3, 2):
             for n in range(2):
                 wa3(d, (x + 4 - d) % 4, n).wait_recv()
@@ -358,13 +386,16 @@
     w_first()
     relay(1)
     forward(0)
+    w_rest()
     share(0)
     relay(2)
+
     forward(1)
     compute(0)
     share(1)
     forward(2)
     w_second()
+    w_rest_z()
     compute(1)
     share(2)
     merge(0)
@@ -418,7 +449,10 @@
         wcopy.wait_send()
 
     for d in range(1, 4):
-        wz(d).wait_send()
+        wz(d, k).wait_send()
+        wc1(d, x).wait_send()
+        wc2(d, y).wait_send()
+        wc3(d, k).wait_send()
         wa2(d, y).wait_send()
         wb2(d, x).wait_send()
         for n in range(2):
@@ -452,9 +486,9 @@
             vmem((128, 1536), BF16),
             vmem((4, 4, 4, 48, 384), BF16),
             dma((3, 2, 3)), dma((3, 4)), dma((3, 4)), dma((3, 4)), dma((3, 4)), dma((3, 4)),
-            dma((3, 2)), dma((3, 3)), dma((32,)),
+            dma((3, 2)), dma((3, 3)), dma((44,)),
             dma((3,)), dma((3,)), dma((3, 4)), dma((3, 4)), dma((3, 4)), dma((3, 4)), dma((3, 4)),
-            dma((2, 3)), dma((3, 3)), dma, dma((7, 4)), dma((4,)),
+            dma((2, 3)), dma((3, 3)), dma, dma((10, 4)), dma((4,)),
         ],
         compiler_params=pltpu.CompilerParams(
             collective_id=0, has_side_effects=True, vmem_limit_bytes=58 << 20

time: 69.6 us -> 68 us (0.977)
  Pallas kernels: 67.8 us -> 66.3 us
    pallas_call x1, Pallas kernels: 67.8 us -> 66.3 us  [on_device(): pl.pallas_call(kernel, out_shape=jax.ShapeDtypeStruct((rows, 768), BF16),...]
where the time goes in v4:
time: 68 us; the launch traced here: 67.9 us
  Pallas kernels  66.3 us (98%)
  local copies, waits for them, and re-layouts  1.62 us (2%)
    pallas_call x1, Pallas kernels, on_device(): pl.pallas_call(kernel, out_shape=jax.ShapeDtypeStruct((rows, 768), BF16),...  66.3 us
    unnamed x1, local copies, waits for them, and re-layouts  1.62 us

profile of v4, /device:TPU:1, one launch (start us, length us, event | category | flops | bytes accessed | tf_op | source)
XLA Modules:
  0.0 67.9 jit_solution(1269266915577123605)
XLA Ops:
  0.0 66.3 %shard_map.64 = bf16[128,768]{1,0:T(8,128)(2,1)} custom-call(bf16[128,768]{1,0:T(8,128)(2,1)} %bitcast.6, bf16[2,128,768]{2,1,0:T(8,128)(2,1)} %bitcast.5, bf16[48,768]{1,0:T(8,128)(2,1)} %bitcast.7, bf16[128,768]{1,0:T(8,128)(2,1)} %latent_hbm.1, s32[1,128]{1,0:T(1,128)} %bitcast.8, s32[1,128]{1,0:T(1,128)} %bitcast.9), custom_call_target="tpu_custom_call" | custom-call | tf_op jit(solution)/shard_map/pallas_call | solution.py:468
  66.3 1.6 %copy.8 = bf16[128,768]{1,0:T(8,128)(2,1)} copy(bf16[128,768]{1,0:T(8,128)(2,1)} %shard_map.64) | data formatting | bytes 393216
